TPU v7x, 128 devices: a whole 4x4x4 slice. The times are simulated.
128 devices in a mesh: dp: 64 (over z, y, x), tensor: 2 (over core).
Axes of the slice: x: 4, y: 4, z: 4, core: 2. Of those that a mesh axis runs over, the one named last changes fastest.
Arguments:
- square_grad: float32 [32, 2359296], P(None, ('dp', 'tensor')), may hold values from -80 to 80
- square_state: float32 [32, 2359296], P(None, ('dp', 'tensor')), may hold values from -6 to 6
- swiglu_grad: float32 [24, 6291456], P(None, ('dp', 'tensor')), may hold values from -80 to 80
- swiglu_state: float32 [24, 6291456], P(None, ('dp', 'tensor')), may hold values from -6 to 6
- square_order: int32 [32], replicated, may hold values from 0 to 31, each once
- swiglu_order: int32 [24], replicated, may hold values from 0 to 23, each once
- owners: int32 [56], replicated, may hold values from 0 to 63, as said below
- vector_values: float32 [172032], P(('dp', 'tensor')), may hold values from -6 to 6
- vector_grad: float32 [172032], P(('dp', 'tensor')), may hold values from -6 to 6
- vector_first: float32 [172032], P(('dp', 'tensor')), may hold values from -4 to 4
- vector_second: float32 [172032], P(('dp', 'tensor')), may hold values from 0.01 to 1
- embed_values: float32 [8192, 1536], P('dp', 'tensor'), may hold values from -6 to 6
- embed_grad: float32 [8192, 1536], P('dp', 'tensor'), may hold values from -6 to 6
- embed_first: float32 [8192, 1536], P('dp', 'tensor'), may hold values from -4 to 4
- embed_second: float32 [8192, 1536], P('dp', 'tensor'), may hold values from 0.01 to 1
- embed_ranges: int32 [16, 2], replicated, may hold values from 0 to 8192, as said below
Outputs:
- square_next: float32 [32, 2359296], P(None, ('dp', 'tensor'))
- swiglu_next: float32 [24, 6291456], P(None, ('dp', 'tensor'))
- square_update: bfloat16 [32, 1536, 1536], P(None, 'dp', 'tensor')
- swiglu_update: bfloat16 [24, 1536, 4096], P(None, 'dp', 'tensor')
- owner_norms: float32 [64], P('dp')
- vector_step: float32 [172032], P(('dp', 'tensor'))
- first_vector: float32 [172032], P(('dp', 'tensor'))
- second_vector: float32 [172032], P(('dp', 'tensor'))
- embed_step: float32 [8192, 1536], P('dp', 'tensor')
- first_embed: float32 [8192, 1536], P('dp', 'tensor')
- second_embed: float32 [8192, 1536], P('dp', 'tensor')
Inputs may be any that keep to these rules, and one draw needn't show every extreme that they name: Different matrices have different owners. `square_order`: each matrix once. `swiglu_order`: each matrix once. `embed_ranges`: start < end in every row.
All inputs are finite; a program needn't handle non-finite values.
Results may differ from a plain program's by a relative error of at most 0.0065.
Values may be sent and summed in bfloat16 or wider, within the bound.
A program may use at most 128 MiB of HBM per device.

v0:
```python
import math
import jax
import jax.numpy as jnp
from jax import lax
from jax.sharding import PartitionSpec as P

D = 1536
FF = 4096
NS_STEPS = 2
QUINTIC_LINEAR = 3.4445
QUINTIC_CUBIC = -4.775
QUINTIC_FIFTH = 2.0315
MOMENTUM = 0.95
BIAS_FIRST = 1.0 - 0.9**10
BIAS_SECOND = 1.0 - 0.95**10


def momentum_terms(gradient, state):
    state_next = MOMENTUM * state + gradient
    return (state_next, (gradient + MOMENTUM * state_next).astype(jnp.bfloat16))


def adamw_terms(values, gradient, first, second):
    first_next = 0.9 * first + 0.1 * gradient
    second_next = 0.95 * second + 0.05 * gradient * gradient
    direction = (
        first_next / BIAS_FIRST / (jnp.sqrt(second_next / BIAS_SECOND) + 1e-08) + 0.1 * values
    )
    return (direction, first_next, second_next)


def table_lookup(table, positions):
    matches = positions[:, None] == jnp.arange(table.shape[0], dtype=jnp.int32)[None, :]
    return jnp.sum(jnp.where(matches, table[None, :], 0), axis=1)


def select_pieces(pieces, piece_owner, targets):
    matched = piece_owner[None, :] == targets[:, None]
    chosen = jnp.sum(
        jnp.where(matched, jnp.arange(piece_owner.shape[0], dtype=jnp.int32)[None, :], 0), axis=1
    )
    present = jnp.any(matched, axis=1)
    picked = jnp.where(present[:, None, None, None], pieces[chosen], jnp.zeros((), jnp.bfloat16))
    return (picked, chosen, present)


def local(
    square_grad,
    square_state,
    swiglu_grad,
    swiglu_state,
    square_order,
    swiglu_order,
    owners,
    vector_values,
    vector_grad,
    vector_first,
    vector_second,
    embed_values,
    embed_grad,
    embed_first,
    embed_second,
    embed_ranges,
):
    wide_count = lax.axis_size("dp")
    split_count = lax.axis_size("tensor")
    wide_index = lax.axis_index("dp")
    square_count = square_grad.shape[0]
    swiglu_count = swiglu_grad.shape[0]
    flat_rows = D // (wide_count * split_count)
    slot_width = FF // split_count
    square_width = D // split_count
    square_next, square_send = momentum_terms(square_grad, square_state)
    swiglu_next, swiglu_send = momentum_terms(swiglu_grad, swiglu_state)
    square_pieces = square_send.reshape(
        square_count, flat_rows, split_count, square_width
    ).transpose(0, 2, 1, 3)
    swiglu_pieces = swiglu_send.reshape(swiglu_count, flat_rows, split_count, slot_width).transpose(
        0, 2, 1, 3
    )
    square_owner = table_lookup(owners[:square_count], square_order)
    swiglu_owner = table_lookup(owners[square_count:], swiglu_order)
    targets = jnp.arange(wide_count, dtype=jnp.int32)
    square_mine = jnp.any(square_owner == wide_index)
    owned = square_mine | jnp.any(swiglu_owner == wide_index)
    factor = jnp.where(square_mine, jnp.float32(math.sqrt(D)), jnp.float32(math.sqrt(FF)))
    widened = jnp.pad(square_pieces, ((0, 0), (0, 0), (0, 0), (0, slot_width - square_width)))
    all_pieces = jnp.concatenate([widened, swiglu_pieces], axis=0)
    slot_owner = jnp.concatenate([square_owner, swiglu_owner])
    outgoing, chosen, present = select_pieces(all_pieces, slot_owner, targets)
    arrived = lax.all_to_all(
        outgoing.reshape(D, slot_width), ("dp", "tensor"), split_axis=0, concat_axis=0, tiled=True
    )
    iterate = arrived
    first_scale = jnp.float32(1.0)
    for round_index in range(NS_STEPS):
        current = iterate
        gram_part = lax.psum_scatter(
            jnp.einsum("rc,sc->rs", current, current, preferred_element_type=jnp.float32),
            "tensor",
            scatter_dimension=0,
            tiled=True,
        )
        if round_index == 0:
            squares_total = lax.psum(jnp.sum(gram_part * gram_part), "tensor")
            gram_scale = jnp.sqrt(squares_total) + 1e-06
            first_scale = gram_scale
        else:
            gram_scale = jnp.float32(1.0)
        normed_part = (gram_part / gram_scale).astype(jnp.bfloat16)
        squared = jnp.dot(
            normed_part,
            lax.all_gather(normed_part, "tensor", axis=0, tiled=True),
            preferred_element_type=jnp.float32,
        )
        polynomial = (
            QUINTIC_CUBIC * normed_part.astype(jnp.float32) + QUINTIC_FIFTH * squared
        ).astype(jnp.bfloat16)
        product = jnp.dot(
            lax.all_gather(polynomial, "tensor", axis=0, tiled=True),
            current,
            preferred_element_type=jnp.float32,
        )
        mixed = (QUINTIC_LINEAR * current.astype(jnp.float32) + product) / jnp.sqrt(gram_scale)
        if round_index == NS_STEPS - 1:
            iterate = (factor * mixed).astype(jnp.bfloat16)
        else:
            iterate = mixed.astype(jnp.bfloat16)
    returned = lax.all_to_all(
        iterate.reshape(wide_count, D // wide_count, slot_width),
        "dp",
        split_axis=0,
        concat_axis=0,
        tiled=True,
    )
    square_update = returned[owners[:square_count]][:, :, :square_width]
    swiglu_update = returned[owners[square_count:]]
    owner_norms = jnp.where(owned, 0.5 * jnp.log(first_scale), 0.0).reshape(1)
    vector_step, first_vector, second_vector = adamw_terms(
        vector_values, vector_grad, vector_first, vector_second
    )
    embed_rows = embed_values.shape[0]
    row_numbers = wide_index * embed_rows + jnp.arange(embed_rows, dtype=jnp.int32)
    inside = (row_numbers[:, None] >= embed_ranges[None, :, 0]) & (
        row_numbers[:, None] < embed_ranges[None, :, 1]
    )
    row_live = jnp.sum(inside.astype(jnp.int32), axis=1) > 0
    direction, first_next, second_next = adamw_terms(
        embed_values, embed_grad, embed_first, embed_second
    )
    embed_step = jnp.where(row_live[:, None], direction, 0.0)
    first_embed = jnp.where(row_live[:, None], first_next, embed_first)
    second_embed = jnp.where(row_live[:, None], second_next, embed_second)
    return (
        square_next,
        swiglu_next,
        square_update,
        swiglu_update,
        owner_norms,
        vector_step,
        first_vector,
        second_vector,
        embed_step,
        first_embed,
        second_embed,
    )


def solution(mesh):
    placed = (
        P(None, ("dp", "tensor")),
        P(None, ("dp", "tensor")),
        P(None, ("dp", "tensor")),
        P(None, ("dp", "tensor")),
        P(),
        P(),
        P(),
        P(("dp", "tensor")),
        P(("dp", "tensor")),
        P(("dp", "tensor")),
        P(("dp", "tensor")),
        P("dp", "tensor"),
        P("dp", "tensor"),
        P("dp", "tensor"),
        P("dp", "tensor"),
        P(),
    )
    return jax.shard_map(
        local,
        mesh=mesh,
        in_specs=placed,
        out_specs=(
            P(None, ("dp", "tensor")),
            P(None, ("dp", "tensor")),
            P(None, "dp", "tensor"),
            P(None, "dp", "tensor"),
            P("dp"),
            P(("dp", "tensor")),
            P(("dp", "tensor")),
            P(("dp", "tensor")),
            P("dp", "tensor"),
            P("dp", "tensor"),
            P("dp", "tensor"),
        ),
        check_vma=False,
    )
```

profile of v0, /device:TPU:4, one launch (start us, length us, event | category | flops | bytes accessed | tf_op | source)
XLA Modules:
  0.0 515.0 jit_solution(1465619128677415151)
XLA Ops:
  7.2 0.7 compare_select_fusion.1
  8.0 0.7 compare_select_fusion.2
  8.6 0.8 select_reduce_fusion.2
  9.5 0.8 select_reduce_fusion.1
  10.3 0.1 pad_add_fusion
  10.4 0.1 select_reduce_fusion
  10.5 0.3 copy-done.11
  10.8 0.1 fusion.4
  10.9 4.2 add_convert_fusion.3
  15.1 0.9 reshape.74
  16.0 7.5 %add_convert_fusion.2 = (bf16[24,49152]{1,0:T(8,128)(2,1)}, f32[24,49152]{1,0:T(8,128)}) fusion(f32[24,49152]{1,0:T(8,128)} %param.18, f32[24,49152]{1,0:T(8,128)} %param.19), kind=kLoop, calls=%fused_computation.12 | loop fusion | flops 5898240 | bytes 16515072 | tf_op jit(solution)/shard_map/convert_element_type | solution.py:20
  23.5 3.5 reshape.75
  27.0 5.3 %fusion = bf16[56,2,12,2048]{3,1,2,0:T(2,128)(2,1)} fusion(bf16[32,2,12,768]{3,1,2,0:T(2,128)(2,1)S(1)} %bitcast.28, bf16[24,2,12,2048]{3,1,2,0:T(2,128)(2,1)S(1)} %bitcast.26), kind=kLoop, calls=%fused_computation.7 | loop fusion | flops 16515072 | bytes 9043968 | tf_op jit(solution)/shard_map/concatenate | solution.py:88
  32.3 17.6 %gather_fusion = bf16[64,2,12,2048]{3,1,2,0:T(2,128)(2,1)} fusion(bf16[56,2,12,2048]{3,1,2,0:T(2,128)(2,1)} %fusion, s32[1024]{0:T(1024)S(1)} %pad_clamp_fusion.2), kind=kCustom, calls=%fused_computation | custom fusion | bytes 12583168 | tf_op jit(solution)/shard_map/gather | solution.py:43
  49.9 9.4 %copy.29 = bf16[64,2,12,2048]{3,2,1,0:T(8,128)(2,1)} copy(bf16[64,2,12,2048]{3,1,2,0:T(2,128)(2,1)} %gather_fusion) | data formatting | bytes 12582912 | tf_op jit(solution)/shard_map/gather | solution.py:43
  59.4 0.2 broadcast_in_dim.100
  59.5 7.2 %bitcast_select_fusion = bf16[128,12,2048]{2,1,0:T(8,128)(2,1)} fusion(bf16[64,2,12,2048]{3,2,1,0:T(8,128)(2,1)} %copy.29, pred[128]{0:T(512)(128)(4,1)S(1)} %broadcast_in_dim.100), kind=kLoop, calls=%fused_computation.6 | loop fusion | flops 3145728 | bytes 12583040 | tf_op jit(solution)/shard_map/jit(_where)/select_n | solution.py:43
  66.8 107.0 %all_to_all.14 = bf16[128,12,2048]{2,1,0:T(8,128)(2,1)} all-to-all(bf16[128,12,2048]{2,1,0:T(8,128)(2,1)} %bitcast_select_fusion), channel_id=1, replica_groups=mesh['dp'=64,'tensor'=2] {'dp','tensor'}, dimensions={0} | all-to-all | bytes 12582912 | tf_op jit(solution)/shard_map/all_to_all | solution.py:91
  173.8 10.7 %all_to_all.10 = bf16[1536,2048]{1,0:T(8,128)(2,1)} reshape(bf16[128,12,2048]{2,1,0:T(8,128)(2,1)} %all_to_all.14) | data formatting | bytes 12582912 | tf_op jit(solution)/shard_map/all_to_all | solution.py:91
  184.5 16.2 %fusion.8 = f32[1536,1536]{1,0:T(8,128)} fusion(bf16[1536,2048]{1,0:T(8,128)(2,1)} %all_to_all.10), kind=kOutput, calls=%fused_computation.48 | convolution fusion | flops 9663676416 | bytes 15728640 | tf_op jit(solution)/shard_map/rc,sc->rs/dot_general | solution.py:99
  200.8 18.6 %reduce-scatter.3.cloned.1.call-done = f32[768,1536]{1,0:T(8,128)} async-done(((f32[1536,1536]{1,0:T(8,128)}), f32[768,1536]{1,0:T(8,128)}) %reduce-scatter.3.cloned.1.call-update) | async-done | bytes 4718608 | tf_op jit(solution)/shard_map/reduce_scatter | solution.py:98
  219.4 4.2 multiply_reduce_fusion
  223.5 3.1 psum.7
  227.3 4.3 divide_convert_fusion.1
  231.7 18.6 %all-gather.5.cloned.1.call-done = bf16[1536,1536]{1,0:T(8,128)(2,1)} async-done(((bf16[768,1536]{1,0:T(8,128)(2,1)}), bf16[1536,1536]{1,0:T(8,128)(2,1)}) %all-gather.5.cloned.1.call-update) | async-done | bytes 4718608 | tf_op jit(solution)/shard_map/all_gather | solution.py:113
  250.3 9.1 %add_convert_fusion.1 = bf16[768,1536]{1,0:T(8,128)(2,1)} fusion(bf16[768,1536]{1,0:T(8,128)(2,1)} %divide_convert_fusion.1, bf16[1536,1536]{1,0:T(8,128)(2,1)} %all-gather.5.cloned.1.call-done), kind=kOutput, calls=%fused_computation.9 | convolution fusion | flops 3629776896 | bytes 9437184 | tf_op jit(solution)/shard_map/dot_general | solution.py:111
  259.4 0.2 reduce-scatter.5.cloned.1.call-start
  259.7 18.4 %all-gather.7.cloned.1.call-done = bf16[1536,1536]{1,0:T(8,128)(2,1)} async-done(((bf16[768,1536]{1,0:T(8,128)(2,1)}), bf16[1536,1536]{1,0:T(8,128)(2,1)}) %all-gather.7.cloned.1.call-update) | async-done | bytes 4718608 | tf_op jit(solution)/shard_map/all_gather | solution.py:120
  278.1 14.9 %divide_convert_fusion = bf16[1536,2048]{1,0:T(8,128)(2,1)S(1)} fusion(bf16[1536,2048]{1,0:T(8,128)(2,1)} %all_to_all.10, bf16[1536,1536]{1,0:T(8,128)(2,1)} %all-gather.7.cloned.1.call-done, f32[]{:T(128)S(6)} %sqrt.13), kind=kOutput, calls=%fused_computation.5 | convolution fusion | flops 9679405056 | bytes 17301508 | tf_op jit(solution)/shard_map/dot_general | solution.py:119
  293.0 2.7 copy-done.13
  295.6 12.7 %fusion.9 = f32[1536,1536]{1,0:T(8,128)} fusion(bf16[1536,2048]{1,0:T(8,128)(2,1)S(1)} %divide_convert_fusion), kind=kOutput, calls=%fused_computation.49 | convolution fusion | flops 9663676416 | bytes 15728640 | tf_op jit(solution)/shard_map/rc,sc->rs/dot_general | solution.py:99
  308.4 22.0 %reduce-scatter.5.cloned.1.call-done = f32[768,1536]{1,0:T(8,128)} async-done(((f32[1536,1536]{1,0:T(8,128)}), f32[768,1536]{1,0:T(8,128)}) %reduce-scatter.5.cloned.1.call-update) | async-done | bytes 4718608 | tf_op jit(solution)/shard_map/reduce_scatter | solution.py:98
  330.4 4.0 convert_element_type.49
  334.5 0.3 all-gather.11.cloned.1.call-start
  334.7 18.5 %all-gather.9.cloned.1.call-done = bf16[1536,1536]{1,0:T(8,128)(2,1)} async-done(((bf16[768,1536]{1,0:T(8,128)(2,1)}), bf16[1536,1536]{1,0:T(8,128)(2,1)}) %all-gather.9.cloned.1.call-update) | async-done | bytes 4718608 | tf_op jit(solution)/shard_map/all_gather | solution.py:113
  353.2 9.1 %add_convert_fusion = bf16[768,1536]{1,0:T(8,128)(2,1)} fusion(bf16[768,1536]{1,0:T(8,128)(2,1)} %convert_element_type.49, bf16[1536,1536]{1,0:T(8,128)(2,1)} %all-gather.9.cloned.1.call-done), kind=kOutput, calls=%fused_computation.8 | convolution fusion | flops 3629776896 | bytes 9437184 | tf_op jit(solution)/shard_map/dot_general | solution.py:111
  362.3 0.6 compare_reduce_fusion.1
  363.6 17.4 %all-gather.11.cloned.1.call-done = bf16[1536,1536]{1,0:T(8,128)(2,1)} async-done(((bf16[768,1536]{1,0:T(8,128)(2,1)}), bf16[1536,1536]{1,0:T(8,128)(2,1)}) %all-gather.11.cloned.1.call-update) | async-done | bytes 4718608 | tf_op jit(solution)/shard_map/all_gather | solution.py:120
  380.9 16.6 %multiply_convert_fusion = bf16[1536,2048]{1,0:T(8,128)(2,1)} fusion(bf16[1536,2048]{1,0:T(8,128)(2,1)} %copy-done.13, bf16[1536,1536]{1,0:T(8,128)(2,1)} %all-gather.11.cloned.1.call-done, f32[]{:T(128)S(6)} %select_n.54), kind=kOutput, calls=%fused_computation.4 | convolution fusion | flops 9679405056 | bytes 17301508 | tf_op jit(solution)/shard_map/dot_general | solution.py:119
  397.6 10.7 %all-to-all-start.1 = ((bf16[64,24,2048]{2,1,0:T(8,128)(2,1)}), bf16[64,24,2048]{2,1,0:T(8,128)(2,1)}, u32[]{:S(2)}, u32[]{:S(2)}) async-start(bf16[64,24,2048]{2,1,0:T(8,128)(2,1)} %bitcast.27), calls=%async_computation.3 | async-start | bytes 12582912 | tf_op jit(solution)/shard_map/all_to_all | solution.py:129
  408.4 0.6 compare_reduce_fusion
  410.4 0.1 convert_reduce_fusion
  410.5 0.6 multiply_add_fusion.3
  411.1 1.4 fusion.3
  412.6 84.5 %all-to-all-done.1 = bf16[64,24,2048]{2,1,0:T(8,128)(2,1)} async-done(((bf16[64,24,2048]{2,1,0:T(8,128)(2,1)}), bf16[64,24,2048]{2,1,0:T(8,128)(2,1)}, u32[]{:S(2)}, u32[]{:S(2)}) %all-to-all-start.1) | async-done | bytes 6291488 | tf_op jit(solution)/shard_map/all_to_all | solution.py:129
  497.1 3.5 gather_fusion.1
  500.7 1.1 slice.28
  501.8 5.0 gather_fusion.2
  (44 shorter events, 0.4 us)
Async XLA Ops:
  7.2 212.2 %reduce-scatter.3.cloned.1.call-start = ((), (), s32[]{:S(2)}) async-start(), calls=%async_computation.4 | async-start | bytes 14155776 | tf_op jit(solution)/shard_map/reduce_scatter | solution.py:98
  9.4 1.0 copy-start.9
  10.3 0.5 copy-start.11
  200.7 49.6 %all-gather.5.cloned.1.call-start = ((), (), s32[]{:S(2)}) async-start(), calls=%async_computation.5 | async-start | bytes 7077888 | tf_op jit(solution)/shard_map/all_gather | solution.py:113
  231.6 46.4 %all-gather.7.cloned.1.call-start = ((), (), s32[]{:S(2)}) async-start(), calls=%async_computation.6 | async-start | bytes 7077888 | tf_op jit(solution)/shard_map/all_gather | solution.py:120
  259.4 71.0 %reduce-scatter.5.cloned.1.call-start = ((), (), s32[]{:S(2)}) async-start(), calls=%async_computation.7 | async-start | bytes 14155776 | tf_op jit(solution)/shard_map/reduce_scatter | solution.py:98
  293.0 2.7 copy-start.13
  308.4 44.8 %all-gather.9.cloned.1.call-start = ((), (), s32[]{:S(2)}) async-start(), calls=%async_computation.8 | async-start | bytes 7077888 | tf_op jit(solution)/shard_map/all_gather | solution.py:113
  334.5 27.8 %copy-start.12 = (s32[32]{0:T(128)S(1)}, s32[32]{0:T(128)}, u32[]{:S(2)}) copy-start(s32[32]{0:T(128)} %copy-done.11) | copy-start | bytes 388
  334.5 46.5 %all-gather.11.cloned.1.call-start = ((), (), s32[]{:S(2)}) async-start(), calls=%async_computation.9 | async-start | bytes 7077888 | tf_op jit(solution)/shard_map/all_gather | solution.py:120
  397.5 10.8 %copy-start.10 = (s32[24]{0:T(128)S(1)}, s32[24]{0:T(128)}, u32[]{:S(2)}) copy-start(s32[24]{0:T(128)} %copy-done.9) | copy-start | bytes 292
  397.6 12.8 %copy-start.8 = (s32[16,2]{0,1:T(2,128)S(1)}, s32[16,2]{0,1:T(2,128)}, u32[]{:S(2)}) copy-start(s32[16,2]{0,1:T(2,128)} %param.31) | copy-start | bytes 388
  397.6 12.9 %copy-start.4 = (f32[1344]{0:T(1024)S(1)}, f32[1344]{0:T(1024)}, u32[]{:S(2)}) copy-start(f32[1344]{0:T(1024)} %param.23) | copy-start | bytes 16132
  397.6 12.9 %copy-start.5 = (f32[1344]{0:T(1024)S(1)}, f32[1344]{0:T(1024)}, u32[]{:S(2)}) copy-start(f32[1344]{0:T(1024)} %param.24) | copy-start | bytes 16132
  397.6 12.9 %copy-start.6 = (f32[1344]{0:T(1024)S(1)}, f32[1344]{0:T(1024)}, u32[]{:S(2)}) copy-start(f32[1344]{0:T(1024)} %param.25) | copy-start | bytes 16132
  397.6 12.9 %copy-start.7 = (f32[1344]{0:T(1024)S(1)}, f32[1344]{0:T(1024)}, u32[]{:S(2)}) copy-start(f32[1344]{0:T(1024)} %param.26) | copy-start | bytes 16132
  397.6 13.5 %copy-start = (f32[128,768]{1,0:T(8,128)S(1)}, f32[128,768]{1,0:T(8,128)}, u32[]{:S(2)}) copy-start(f32[128,768]{1,0:T(8,128)} %param.30) | copy-start | bytes 1179652
  397.6 13.5 %copy-start.1 = (f32[128,768]{1,0:T(8,128)S(1)}, f32[128,768]{1,0:T(8,128)}, u32[]{:S(2)}) copy-start(f32[128,768]{1,0:T(8,128)} %param.28) | copy-start | bytes 1179652
  397.6 13.5 %copy-start.2 = (f32[128,768]{1,0:T(8,128)S(1)}, f32[128,768]{1,0:T(8,128)}, u32[]{:S(2)}) copy-start(f32[128,768]{1,0:T(8,128)} %param.27) | copy-start | bytes 1179652
  397.6 13.5 %copy-start.3 = (f32[128,768]{1,0:T(8,128)S(1)}, f32[128,768]{1,0:T(8,128)}, u32[]{:S(2)}) copy-start(f32[128,768]{1,0:T(8,128)} %param.29) | copy-start | bytes 1179652
  397.6 99.5 %all-to-all-start.1 = ((bf16[64,24,2048]{2,1,0:T(8,128)(2,1)}), bf16[64,24,2048]{2,1,0:T(8,128)(2,1)}, u32[]{:S(2)}, u32[]{:S(2)}) async-start(bf16[64,24,2048]{2,1,0:T(8,128)(2,1)} %bitcast.27), calls=%async_computation.3 | async-start | bytes 12582912 | tf_op jit(solution)/shard_map/all_to_all | solution.py:129
Sparse Core Ops, SparseCore 0:
  200.8 18.4 reduce-scatter.2
  231.8 18.5 all-gather.4
  259.5 18.4 all-gather.6
  308.5 21.8 reduce-scatter.4
  334.6 18.5 all-gather.8
  362.4 18.4 all-gather.10
where the time goes:
time: 524 us; the launch traced here: 515 us
  waiting for transfers between devices  198 us (38%)
  blocking collectives  110 us (21%)
  matrix products  78.6 us (15%)
  local copies, waits for them, and re-layouts  55 us (10%)
  other arithmetic  43.4 us (8%)
  between operations  18.5 us (4%)
  starting transfers between devices  11.3 us (2%)
    all_to_all x1, blocking collectives, local(): lax.all_to_all(outgoing.reshape(D, slot_width), ('dp', 'tensor'), split_a...  107 us
    all_to_all x1, waiting for transfers between devices, local(): lax.all_to_all(iterate.reshape(wide_count, D // wide_count, slot_width),...  84.5 us
    reduce_scatter x2, waiting for transfers between devices, local(): lax.psum_scatter(jnp.einsum('rc,sc->rs', current, current, preferred_elem...  40.6 us
    all_gather x2, waiting for transfers between devices, local(): lax.all_gather(normed_part, 'tensor', axis=0, tiled=True)  37.1 us
    all_gather x2, waiting for transfers between devices, local(): lax.all_gather(polynomial, 'tensor', axis=0, tiled=True)  35.7 us
    dot_general x2, matrix products, local(): jnp.dot(lax.all_gather(polynomial, 'tensor', axis=0, tiled=True), current...  31.5 us
    dot_general x2, matrix products, local(): jnp.einsum('rc,sc->rs', current, current, preferred_element_type=jnp.floa...  29 us
    gather x2, local copies, waits for them, and re-layouts, select_pieces(): pieces[chosen]  27 us
  transfers between devices with their start and end apart: 7, of which 7 were waited for; matrix products, arithmetic and copies ran while one was open for 1% of the time, Pallas kernels for 0%

commit v1 on v0

--- a/solution.py
+++ b/solution.py
@@ -13,6 +13,11 @@
 MOMENTUM = 0.95
 BIAS_FIRST = 1.0 - 0.9**10
 BIAS_SECOND = 1.0 - 0.95**10
+
+
+def check_sources_all(packet):
+    part_next = jnp.concatenate([packet for _ in range(lax.axis_size("tensor"))], axis=0)
+    return lax.all_to_all(part_next, "tensor", 0, 0, tiled=True)
 
 
 def momentum_terms(gradient, state):
@@ -109,9 +114,7 @@
             gram_scale = jnp.float32(1.0)
         normed_part = (gram_part / gram_scale).astype(jnp.bfloat16)
         squared = jnp.dot(
-            normed_part,
-            lax.all_gather(normed_part, "tensor", axis=0, tiled=True),
-            preferred_element_type=jnp.float32,
+            normed_part, check_sources_all(normed_part), preferred_element_type=jnp.float32
         )
         polynomial = (
             QUINTIC_CUBIC * normed_part.astype(jnp.float32) + QUINTIC_FIFTH * squared

time: 524 us -> 483 us (0.922); the launches traced: 515 us -> 481 us
  waiting for transfers between devices: 198 us -> 161 us
  blocking collectives: 110 us -> 125 us
  matrix products: 78.6 us -> 70.6 us
    all_gather x2 -> x0, waiting for transfers between devices: 37.1 us -> none  [local(): lax.all_gather(normed_part, 'tensor', axis=0, tiled=True)]
    all_to_all x0 -> x2, blocking collectives: none -> 15.1 us  [check_sources_all(): return lax.all_to_all(part_next, 'tensor', 0, 0, tiled=True)]
    dot_general x2, matrix products: 18.2 us -> 10.2 us  [local(): jnp.dot(normed_part, check_sources_all(normed_part), preferred_element_ty...]
  transfers between devices with their start and end apart: 7 -> 5, of which waited for: 7 -> 5; matrix products, arithmetic and copies ran while one was open for 1% -> 1% of each run, Pallas kernels for 0% -> 0%
where the time goes in v1:
time: 483 us; the launch traced here: 481 us
  waiting for transfers between devices  161 us (33%)
  blocking collectives  125 us (26%)
  matrix products  70.6 us (15%)
  local copies, waits for them, and re-layouts  55 us (11%)
  other arithmetic  41.3 us (9%)
  between operations  17.9 us (4%)
  starting transfers between devices  11.1 us (2%)
    all_to_all x1, blocking collectives, local(): lax.all_to_all(outgoing.reshape(D, slot_width), ('dp', 'tensor'), split_a...  107 us
    all_to_all x1, waiting for transfers between devices, local(): lax.all_to_all(iterate.reshape(wide_count, D // wide_count, slot_width),...  84.5 us
    reduce_scatter x2, waiting for transfers between devices, local(): lax.psum_scatter(jnp.einsum('rc,sc->rs', current, current, preferred_elem...  40.5 us
    all_gather x2, waiting for transfers between devices, local(): lax.all_gather(polynomial, 'tensor', axis=0, tiled=True)  35.7 us
    dot_general x2, matrix products, local(): jnp.dot(lax.all_gather(polynomial, 'tensor', axis=0, tiled=True), current...  31.5 us
    dot_general x2, matrix products, local(): jnp.einsum('rc,sc->rs', current, current, preferred_element_type=jnp.floa...  29 us
    gather x2, local copies, waits for them, and re-layouts, select_pieces(): pieces[chosen]  27 us
    all_to_all x2, blocking collectives, check_sources_all(): return lax.all_to_all(part_next, 'tensor', 0, 0, tiled=True)  15.1 us
  transfers between devices with their start and end apart: 5, of which 5 were waited for; matrix products, arithmetic and copies ran while one was open for 1% of the time, Pallas kernels for 0%

profile of v1, /device:TPU:4, one launch (start us, length us, event | category | flops | bytes accessed | tf_op | source)
XLA Modules:
  0.0 481.5 jit_solution(7356289580619887734)
XLA Ops:
  7.2 0.7 compare_select_fusion.1
  8.0 0.7 compare_select_fusion.2
  8.6 0.8 select_reduce_fusion.2
  9.5 0.8 select_reduce_fusion.1
  10.4 0.1 select_reduce_fusion
  10.5 0.3 copy-done.11
  10.8 0.1 fusion.4
  10.9 4.2 add_convert_fusion.3
  15.1 0.9 reshape.78
  16.0 7.5 %add_convert_fusion.2 = (bf16[24,49152]{1,0:T(8,128)(2,1)}, f32[24,49152]{1,0:T(8,128)}) fusion(f32[24,49152]{1,0:T(8,128)} %param.18, f32[24,49152]{1,0:T(8,128)} %param.19), kind=kLoop, calls=%fused_computation.14 | loop fusion | flops 5898240 | bytes 16515072 | tf_op jit(solution)/shard_map/convert_element_type | solution.py:25
  23.5 3.5 reshape.79
  27.0 5.3 %fusion = bf16[56,2,12,2048]{3,1,2,0:T(2,128)(2,1)} fusion(bf16[32,2,12,768]{3,1,2,0:T(2,128)(2,1)S(1)} %bitcast.34, bf16[24,2,12,2048]{3,1,2,0:T(2,128)(2,1)S(1)} %bitcast.32), kind=kLoop, calls=%fused_computation.7 | loop fusion | flops 16515072 | bytes 9043968 | tf_op jit(solution)/shard_map/concatenate | solution.py:93
  32.3 17.6 %gather_fusion = bf16[64,2,12,2048]{3,1,2,0:T(2,128)(2,1)} fusion(bf16[56,2,12,2048]{3,1,2,0:T(2,128)(2,1)} %fusion, s32[1024]{0:T(1024)S(1)} %pad_clamp_fusion.2), kind=kCustom, calls=%fused_computation | custom fusion | bytes 12583168 | tf_op jit(solution)/shard_map/gather | solution.py:48
  49.9 9.4 %copy.29 = bf16[64,2,12,2048]{3,2,1,0:T(8,128)(2,1)} copy(bf16[64,2,12,2048]{3,1,2,0:T(2,128)(2,1)} %gather_fusion) | data formatting | bytes 12582912 | tf_op jit(solution)/shard_map/gather | solution.py:48
  59.4 0.2 broadcast_in_dim.100
  59.5 7.2 %bitcast_select_fusion = bf16[128,12,2048]{2,1,0:T(8,128)(2,1)} fusion(bf16[64,2,12,2048]{3,2,1,0:T(8,128)(2,1)} %copy.29, pred[128]{0:T(512)(128)(4,1)S(1)} %broadcast_in_dim.100), kind=kLoop, calls=%fused_computation.6 | loop fusion | flops 3145728 | bytes 12583040 | tf_op jit(solution)/shard_map/jit(_where)/select_n | solution.py:48
  66.7 106.5 %all_to_all.38 = bf16[128,12,2048]{2,1,0:T(8,128)(2,1)} all-to-all(bf16[128,12,2048]{2,1,0:T(8,128)(2,1)} %bitcast_select_fusion), channel_id=1, replica_groups=mesh['dp'=64,'tensor'=2] {'dp','tensor'}, dimensions={0} | all-to-all | bytes 12582912 | tf_op jit(solution)/shard_map/all_to_all | solution.py:96
  173.3 10.7 %all_to_all.26 = bf16[1536,2048]{1,0:T(8,128)(2,1)} reshape(bf16[128,12,2048]{2,1,0:T(8,128)(2,1)} %all_to_all.38) | data formatting | bytes 12582912 | tf_op jit(solution)/shard_map/all_to_all | solution.py:96
  184.0 16.2 %fusion.8 = f32[1536,1536]{1,0:T(8,128)} fusion(bf16[1536,2048]{1,0:T(8,128)(2,1)} %all_to_all.26), kind=kOutput, calls=%fused_computation.50 | convolution fusion | flops 9663676416 | bytes 15728640 | tf_op jit(solution)/shard_map/rc,sc->rs/dot_general | solution.py:104
  200.3 18.6 %reduce-scatter.3.cloned.1.call-done = f32[768,1536]{1,0:T(8,128)} async-done(((f32[1536,1536]{1,0:T(8,128)}), f32[768,1536]{1,0:T(8,128)}) %reduce-scatter.3.cloned.1.call-update) | async-done | bytes 4718608 | tf_op jit(solution)/shard_map/reduce_scatter | solution.py:103
  218.9 4.2 multiply_reduce_fusion
  223.0 3.1 psum.7
  226.8 2.9 divide_convert_fusion.1
  229.7 0.4 pad_maximum_fusion
  230.1 7.5 %all_to_all.39 = bf16[2,768,1536]{2,1,0:T(8,128)(2,1)S(1)} all-to-all(bf16[2,768,1536]{2,1,0:T(8,128)(2,1)S(1)} %bitcast.30), channel_id=1, replica_groups=mesh['dp'=64,'tensor'=2] {'tensor'}, dimensions={0} | all-to-all | bytes 9437184 | tf_op jit(solution)/shard_map/all_to_all | solution.py:20
  237.6 5.1 %add_convert_fusion.1 = bf16[768,1536]{1,0:T(8,128)(2,1)} fusion(bf16[768,1536]{1,0:T(8,128)(2,1)S(1)} %divide_convert_fusion.1, bf16[1536,1536]{1,0:T(8,128)(2,1)S(1)} %bitcast.35), kind=kOutput, calls=%fused_computation.11 | convolution fusion | flops 3629776896 | bytes 9437184 | tf_op jit(solution)/shard_map/dot_general | solution.py:116
  242.7 0.3 reduce-scatter.5.cloned.1.call-start
  243.0 18.3 %all-gather.3.cloned.1.call-done = bf16[1536,1536]{1,0:T(8,128)(2,1)} async-done(((bf16[768,1536]{1,0:T(8,128)(2,1)}), bf16[1536,1536]{1,0:T(8,128)(2,1)}) %all-gather.3.cloned.1.call-update) | async-done | bytes 4718608 | tf_op jit(solution)/shard_map/all_gather | solution.py:123
  261.3 14.9 %divide_convert_fusion = bf16[1536,2048]{1,0:T(8,128)(2,1)S(1)} fusion(bf16[1536,2048]{1,0:T(8,128)(2,1)} %all_to_all.26, bf16[1536,1536]{1,0:T(8,128)(2,1)} %all-gather.3.cloned.1.call-done, f32[]{:T(128)S(6)} %sqrt.13), kind=kOutput, calls=%fused_computation.5 | convolution fusion | flops 9679405056 | bytes 17301508 | tf_op jit(solution)/shard_map/dot_general | solution.py:122
  276.2 2.7 copy-done.13
  278.9 12.7 %fusion.9 = f32[1536,1536]{1,0:T(8,128)} fusion(bf16[1536,2048]{1,0:T(8,128)(2,1)S(1)} %divide_convert_fusion), kind=kOutput, calls=%fused_computation.51 | convolution fusion | flops 9663676416 | bytes 15728640 | tf_op jit(solution)/shard_map/rc,sc->rs/dot_general | solution.py:104
  291.7 22.0 %reduce-scatter.5.cloned.1.call-done = f32[768,1536]{1,0:T(8,128)} async-done(((f32[1536,1536]{1,0:T(8,128)}), f32[768,1536]{1,0:T(8,128)}) %reduce-scatter.5.cloned.1.call-update) | async-done | bytes 4718608 | tf_op jit(solution)/shard_map/reduce_scatter | solution.py:103
  313.7 2.6 convert_element_type.49
  316.3 0.4 pad_maximum_fusion.1
  316.7 7.5 %all_to_all.40 = bf16[2,768,1536]{2,1,0:T(8,128)(2,1)S(1)} all-to-all(bf16[2,768,1536]{2,1,0:T(8,128)(2,1)S(1)} %bitcast.31), channel_id=1, replica_groups=mesh['dp'=64,'tensor'=2] {'tensor'}, dimensions={0} | all-to-all | bytes 9437184 | tf_op jit(solution)/shard_map/all_to_all | solution.py:20
  324.2 5.1 %add_convert_fusion = bf16[768,1536]{1,0:T(8,128)(2,1)} fusion(bf16[768,1536]{1,0:T(8,128)(2,1)S(1)} %convert_element_type.49, bf16[1536,1536]{1,0:T(8,128)(2,1)S(1)} %bitcast.36), kind=kOutput, calls=%fused_computation.10 | convolution fusion | flops 3629776896 | bytes 9437184 | tf_op jit(solution)/shard_map/dot_general | solution.py:116
  329.4 0.6 compare_reduce_fusion.1
  330.7 17.3 %all-gather.5.cloned.1.call-done = bf16[1536,1536]{1,0:T(8,128)(2,1)} async-done(((bf16[768,1536]{1,0:T(8,128)(2,1)}), bf16[1536,1536]{1,0:T(8,128)(2,1)}) %all-gather.5.cloned.1.call-update) | async-done | bytes 4718608 | tf_op jit(solution)/shard_map/all_gather | solution.py:123
  348.0 16.6 %multiply_convert_fusion = bf16[1536,2048]{1,0:T(8,128)(2,1)} fusion(bf16[1536,2048]{1,0:T(8,128)(2,1)} %copy-done.13, bf16[1536,1536]{1,0:T(8,128)(2,1)} %all-gather.5.cloned.1.call-done, f32[]{:T(128)S(6)} %select_n.54), kind=kOutput, calls=%fused_computation.4 | convolution fusion | flops 9679405056 | bytes 17301508 | tf_op jit(solution)/shard_map/dot_general | solution.py:122
  364.7 10.7 %all-to-all-start.3 = ((bf16[64,24,2048]{2,1,0:T(8,128)(2,1)}), bf16[64,24,2048]{2,1,0:T(8,128)(2,1)}, u32[]{:S(2)}, u32[]{:S(2)}) async-start(bf16[64,24,2048]{2,1,0:T(8,128)(2,1)} %bitcast.33), calls=%async_computation.5 | async-start | bytes 12582912 | tf_op jit(solution)/shard_map/all_to_all | solution.py:132
  375.4 0.6 compare_reduce_fusion
  377.4 0.1 convert_reduce_fusion
  377.5 0.6 multiply_add_fusion.3
  378.2 1.4 fusion.3
  379.7 84.5 %all-to-all-done.3 = bf16[64,24,2048]{2,1,0:T(8,128)(2,1)} async-done(((bf16[64,24,2048]{2,1,0:T(8,128)(2,1)}), bf16[64,24,2048]{2,1,0:T(8,128)(2,1)}, u32[]{:S(2)}, u32[]{:S(2)}) %all-to-all-start.3) | async-done | bytes 6291488 | tf_op jit(solution)/shard_map/all_to_all | solution.py:132
  464.2 3.5 gather_fusion.1
  467.7 1.1 slice.28
  468.8 5.0 %gather_fusion.2 = bf16[24,24,2048]{2,1,0:T(8,128)(2,1)} fusion(bf16[64,24,2048]{2,1,0:T(8,128)(2,1)} %all-to-all-done.3, s32[1024]{0:T(1024)S(1)} %pad_clamp_fusion), kind=kCustom, calls=%fused_computation.2 | custom fusion | bytes 4718688 | tf_op jit(solution)/shard_map/gather | solution.py:140
  (42 shorter events, 0.4 us)
Async XLA Ops:
  7.2 211.7 %reduce-scatter.3.cloned.1.call-start = ((), (), s32[]{:S(2)}) async-start(), calls=%async_computation.6 | async-start | bytes 14155776 | tf_op jit(solution)/shard_map/reduce_scatter | solution.py:103
  9.4 1.0 copy-start.9
  10.3 0.5 copy-start.11
  200.2 61.1 %all-gather.3.cloned.1.call-start = ((), (), s32[]{:S(2)}) async-start(), calls=%async_computation.7 | async-start | bytes 7077888 | tf_op jit(solution)/shard_map/all_gather | solution.py:123
  242.7 71.0 %reduce-scatter.5.cloned.1.call-start = ((), (), s32[]{:S(2)}) async-start(), calls=%async_computation.8 | async-start | bytes 14155776 | tf_op jit(solution)/shard_map/reduce_scatter | solution.py:103
  276.2 2.7 copy-start.13
  291.7 56.3 %all-gather.5.cloned.1.call-start = ((), (), s32[]{:S(2)}) async-start(), calls=%async_computation.9 | async-start | bytes 7077888 | tf_op jit(solution)/shard_map/all_gather | solution.py:123
  324.2 5.1 %copy-start.12 = (s32[32]{0:T(128)S(1)}, s32[32]{0:T(128)}, u32[]{:S(2)}) copy-start(s32[32]{0:T(128)} %copy-done.11) | copy-start | bytes 388
  364.6 10.8 %copy-start.10 = (s32[24]{0:T(128)S(1)}, s32[24]{0:T(128)}, u32[]{:S(2)}) copy-start(s32[24]{0:T(128)} %copy-done.9) | copy-start | bytes 292
  364.6 12.8 %copy-start.8 = (s32[16,2]{0,1:T(2,128)S(1)}, s32[16,2]{0,1:T(2,128)}, u32[]{:S(2)}) copy-start(s32[16,2]{0,1:T(2,128)} %param.31) | copy-start | bytes 388
  364.6 12.9 %copy-start.4 = (f32[1344]{0:T(1024)S(1)}, f32[1344]{0:T(1024)}, u32[]{:S(2)}) copy-start(f32[1344]{0:T(1024)} %param.23) | copy-start | bytes 16132
  364.6 12.9 %copy-start.5 = (f32[1344]{0:T(1024)S(1)}, f32[1344]{0:T(1024)}, u32[]{:S(2)}) copy-start(f32[1344]{0:T(1024)} %param.24) | copy-start | bytes 16132
  364.6 12.9 %copy-start.6 = (f32[1344]{0:T(1024)S(1)}, f32[1344]{0:T(1024)}, u32[]{:S(2)}) copy-start(f32[1344]{0:T(1024)} %param.25) | copy-start | bytes 16132
  364.6 12.9 %copy-start.7 = (f32[1344]{0:T(1024)S(1)}, f32[1344]{0:T(1024)}, u32[]{:S(2)}) copy-start(f32[1344]{0:T(1024)} %param.26) | copy-start | bytes 16132
  364.6 13.5 %copy-start = (f32[128,768]{1,0:T(8,128)S(1)}, f32[128,768]{1,0:T(8,128)}, u32[]{:S(2)}) copy-start(f32[128,768]{1,0:T(8,128)} %param.30) | copy-start | bytes 1179652
  364.7 13.5 %copy-start.1 = (f32[128,768]{1,0:T(8,128)S(1)}, f32[128,768]{1,0:T(8,128)}, u32[]{:S(2)}) copy-start(f32[128,768]{1,0:T(8,128)} %param.28) | copy-start | bytes 1179652
  364.7 13.5 %copy-start.2 = (f32[128,768]{1,0:T(8,128)S(1)}, f32[128,768]{1,0:T(8,128)}, u32[]{:S(2)}) copy-start(f32[128,768]{1,0:T(8,128)} %param.27) | copy-start | bytes 1179652
  364.7 13.5 %copy-start.3 = (f32[128,768]{1,0:T(8,128)S(1)}, f32[128,768]{1,0:T(8,128)}, u32[]{:S(2)}) copy-start(f32[128,768]{1,0:T(8,128)} %param.29) | copy-start | bytes 1179652
  364.7 99.5 %all-to-all-start.3 = ((bf16[64,24,2048]{2,1,0:T(8,128)(2,1)}), bf16[64,24,2048]{2,1,0:T(8,128)(2,1)}, u32[]{:S(2)}, u32[]{:S(2)}) async-start(bf16[64,24,2048]{2,1,0:T(8,128)(2,1)} %bitcast.33), calls=%async_computation.5 | async-start | bytes 12582912 | tf_op jit(solution)/shard_map/all_to_all | solution.py:132
Sparse Core Ops, SparseCore 0:
  200.4 18.4 reduce-scatter.2
  242.8 18.4 all-gather.2
  291.8 21.8 reduce-scatter.4
  329.5 18.4 all-gather.4
